TPU v7x, 32 devices: a whole 2x2x4 slice. The times are simulated.
32 devices in a mesh: tm: 16 (over z, y, x), head: 2 (over core).
Axes of the slice: x: 2, y: 2, z: 4, core: 2. Of those that a mesh axis runs over, the one named last changes fastest.
Arguments:
- patches: bfloat16 [192, 256, 1152], P('tm', None, 'head'), may hold values from -6 to 6
- grid_rows: int32 [192], P('tm'), may hold values from 8 to 16
- frame_ids: int32 [192], P('tm'), may hold values from 0 to 191, as said below
- ln_gain: float32 [1152], replicated, may hold values from 0.1 to 1.9
- w_qkv: bfloat16 [3, 1152, 1152], P(None, None, 'head'), may hold values from -5.9514821 to 5.9514821
- w_out: bfloat16 [1152, 1152], P('head'), may hold values from -0.1875 to 0.1875
- w_conn: bfloat16 [1152, 4096], P(None, 'head'), may hold values from -0.1875 to 0.1875
- norm_gain: float32 [4096], replicated, may hold values from 0.1 to 1.9
- w_x: bfloat16 [4096, 4096], P(None, 'head'), may hold values from -0.09375 to 0.09375
- w_b: bfloat16 [4096, 1024], P(None, 'head'), may hold values from -0.09375 to 0.09375
- w_c: bfloat16 [4096, 1024], P(None, 'head'), may hold values from -0.09375 to 0.09375
- w_dt: bfloat16 [4096, 64], P(None, 'head'), may hold values from -0.09375 to 0.09375
- dt_bias: float32 [64], P('head'), may hold values from -1 to 1
- a_log: float32 [64], P('head'), may hold values from -14 to -3.2
- d_skip: float32 [64], P('head'), may hold values from 0.5 to 1.5
- out_gain: float32 [4096], P('head'), may hold values from 0.1 to 1.9
Outputs:
- stream: bfloat16 [12288, 4096], P('tm', 'head')
- ssd_out: bfloat16 [12288, 4096], P('tm', 'head')
Inputs may be any that keep to these rules, and one draw needn't show every extreme that they name: frame_ids is a permutation of the frames; the 12 slots of one tm index hold frames of 12 different time shards, time shard of a frame being frame // 12.
All inputs are finite; a program needn't handle non-finite values.
Results may differ from a plain program's by a relative error of at most 0.013.
Values may be sent and summed in bfloat16 or wider, within the bound.
A program may use at most 128 MiB of HBM per device.

v0:
```python
import jax
import jax.numpy as jnp
from jax import lax
from jax.sharding import PartitionSpec as P

GRID = 16
POOL = 4
VHD = 72
HDIM = 64
STATE = 128
STRETCH = 256
highest = lax.Precision.HIGHEST


def carried_in(value, axis, combine, identity):
    count, position = (lax.axis_size(axis), lax.axis_index(axis))
    everything = jax.tree.map(
        lambda part, kind: lax.all_gather(part.astype(kind), axis),
        value,
        (jnp.bfloat16, jnp.bfloat16),
    )
    start = jax.tree.map(
        lambda part, zero: jnp.broadcast_to(jnp.asarray(zero, part.dtype), part.shape),
        value,
        identity,
    )

    def step(k, before):
        reached = k < position
        new = combine(
            before, jax.tree.map(lambda part, own: part[k].astype(own.dtype), everything, value)
        )
        return jax.tree.map(lambda a, b: jnp.where(reached, a, b), new, before)

    return lax.fori_loop(0, count, step, start)


def layer_norm(rows, gain):
    values = rows.astype(jnp.float32)
    centre = jnp.mean(values, axis=-1, keepdims=True)
    spread = jnp.mean(jnp.square(values - centre), axis=-1, keepdims=True)
    return ((values - centre) * lax.rsqrt(spread + 1e-06) * gain).astype(jnp.bfloat16)


def attend(full_patches, valid_count, ln_gain, w_qkv, w_out):
    frame_count, patch_count, full_width = full_patches.shape
    local_width = w_qkv.shape[2]
    local_heads = local_width // VHD
    normed = layer_norm(full_patches, ln_gain).reshape(frame_count * patch_count, full_width)
    triple = jnp.einsum("rc,mcd->mrd", normed, w_qkv, preferred_element_type=jnp.float32).astype(
        jnp.bfloat16
    )
    triple = triple.reshape(3, frame_count, patch_count, local_heads, VHD)
    scores = jnp.einsum(
        "fqhd,fkhd->fhqk", triple[0], triple[1], preferred_element_type=jnp.float32
    ) * VHD ** (-0.5)
    usable = jnp.arange(patch_count)[None, :] < valid_count[:, None]
    scores = jnp.where(usable[:, None, None, :], scores, -1e30)
    row_max = jnp.max(scores, axis=-1, keepdims=True)
    powered = jnp.exp(scores - row_max)
    weights_soft = (powered / jnp.sum(powered, axis=-1, keepdims=True)).astype(jnp.bfloat16)
    context = jnp.einsum(
        "fhqk,fkhd->fqhd", weights_soft, triple[2], preferred_element_type=jnp.float32
    ).astype(jnp.bfloat16)
    attended = jnp.dot(
        context.reshape(frame_count * patch_count, local_width),
        w_out,
        preferred_element_type=jnp.float32,
    )
    return jnp.mean(attended.reshape(frame_count, patch_count // POOL, POOL, full_width), axis=2)


def bucket_frames(owned, frame_ids, shards):
    frame_count = owned.shape[0]
    target = frame_ids // frame_count
    onehot = target[None, :] == jnp.arange(shards)[:, None]
    outgoing = jnp.einsum(
        "tf,fpc->tpc", onehot.astype(owned.dtype), owned, preferred_element_type=jnp.float32
    ).astype(owned.dtype)
    labels = jnp.sum(jnp.where(onehot, frame_ids[None, :] + 1, 0), axis=1)
    return (outgoing, labels)


def place_frames(incoming, arrived, frame_count):
    first_frame = lax.axis_index("tm") * frame_count
    local_frame = arrived - 1 - first_frame
    onehot = jnp.arange(frame_count)[:, None] == local_frame[None, :]
    placed = jnp.einsum(
        "ft,tpc->fpc", onehot.astype(incoming.dtype), incoming, preferred_element_type=jnp.float32
    ).astype(incoming.dtype)
    return placed.reshape(frame_count * incoming.shape[1], incoming.shape[2])


def project(stream_rows, norm_gain, w_x, w_b, w_c, w_dt, dt_bias, a_log):
    values = stream_rows.astype(jnp.float32)
    normed = (
        values * lax.rsqrt(jnp.mean(values * values, axis=-1, keepdims=True) + 1e-05) * norm_gain
    ).astype(jnp.bfloat16)
    inner_rows = jnp.dot(normed, w_x, preferred_element_type=jnp.float32).astype(jnp.bfloat16)
    write_keys = jnp.dot(normed, w_b, preferred_element_type=jnp.float32).astype(jnp.bfloat16)
    read_keys = jnp.dot(normed, w_c, preferred_element_type=jnp.float32).astype(jnp.bfloat16)
    step_size = jax.nn.softplus(jnp.dot(normed, w_dt, preferred_element_type=jnp.float32) + dt_bias)
    log_decay = -jnp.exp(a_log) * step_size
    return (inner_rows, write_keys, read_keys, step_size, log_decay)


def ssd_stretch(inner_rows, write_keys, read_keys, step_size, log_decay, d_skip, state):
    length = inner_rows.shape[0]
    head_count = step_size.shape[1]
    groups = write_keys.shape[1] // STATE
    per_group = head_count // groups
    cumul = jnp.cumsum(log_decay, axis=0)
    scaled = (
        inner_rows.astype(jnp.float32).reshape(length, head_count, HDIM) * step_size[:, :, None]
    )
    writers = write_keys.astype(jnp.float32).reshape(length, groups, STATE)
    readers = read_keys.astype(jnp.float32).reshape(length, groups, STATE)
    intersection = jnp.einsum("tgn,sgn->gts", readers, writers, precision=highest)
    causal = (jnp.arange(length)[:, None] >= jnp.arange(length)[None, :])[:, :, None]
    spans = cumul[:, None, :] - cumul[None, :, :]
    decays = jnp.where(causal, jnp.exp(jnp.where(causal, spans, 0.0)), 0.0)
    mixing = jnp.repeat(intersection, per_group, axis=0) * jnp.transpose(decays, (2, 0, 1))
    within = jnp.einsum("hts,shp->thp", mixing, scaled, precision=highest)
    carried = (
        jnp.einsum(
            "tgn,gkpn->tgkp",
            readers,
            state.reshape(groups, per_group, HDIM, STATE),
            precision=highest,
        ).reshape(length, head_count, HDIM)
        * jnp.exp(cumul)[:, :, None]
    )
    remaining = jnp.exp(cumul[-1][None, :] - cumul)
    fresh_state = jnp.einsum(
        "sgkp,sgn->gkpn",
        (scaled * remaining[:, :, None]).reshape(length, groups, per_group, HDIM),
        writers,
        precision=highest,
    ).reshape(head_count, HDIM, STATE)
    new_state = jnp.exp(cumul[-1])[:, None, None] * state + fresh_state
    outputs = (
        within
        + carried
        + d_skip[None, :, None] * inner_rows.astype(jnp.float32).reshape(length, head_count, HDIM)
    )
    return (outputs, new_state, cumul)


def group_norm(outputs, out_gain, groups):
    length = outputs.shape[0]
    grouped = outputs.reshape(length, groups, -1)
    normed = grouped * lax.rsqrt(jnp.mean(grouped * grouped, axis=-1, keepdims=True) + 1e-05)
    return (normed.reshape(length, -1) * out_gain).astype(jnp.bfloat16)


def combine_states(earlier, later):
    return (earlier[0] + later[0], jnp.exp(later[0])[:, None, None] * earlier[1] + later[1])


def on_device(
    patches,
    grid_rows,
    frame_ids,
    ln_gain,
    w_qkv,
    w_out,
    w_conn,
    norm_gain,
    w_x,
    w_b,
    w_c,
    w_dt,
    dt_bias,
    a_log,
    d_skip,
    out_gain,
):
    frame_count, patch_count, slice_width = patches.shape
    tokens_frame = patch_count // POOL
    shards = lax.axis_size("tm")
    full_patches = lax.all_gather(patches, "head", axis=2, tiled=True)
    full_width = full_patches.shape[2]
    valid_count = grid_rows * GRID
    attn_pooled = attend(full_patches, valid_count, ln_gain, w_qkv, w_out)
    kept_tokens = (jnp.arange(tokens_frame)[None, :] * POOL < valid_count[:, None])[:, :, None]
    summed_attn = lax.psum(attn_pooled, "head")
    pooled_patches = jnp.mean(
        full_patches.astype(jnp.float32).reshape(frame_count, tokens_frame, POOL, full_width),
        axis=2,
    )
    vision = jnp.where(kept_tokens, pooled_patches + summed_attn, 0.0).astype(jnp.bfloat16)
    projected = jnp.dot(
        vision.reshape(frame_count * tokens_frame, full_width),
        w_conn,
        preferred_element_type=jnp.float32,
    ).astype(jnp.bfloat16)
    outgoing, labels = bucket_frames(
        projected.reshape(frame_count, tokens_frame, w_conn.shape[1]), frame_ids, shards
    )
    incoming, arrived = (
        lax.all_to_all(outgoing, "tm", split_axis=0, concat_axis=0, tiled=True),
        lax.all_to_all(labels, "tm", split_axis=0, concat_axis=0, tiled=True),
    )
    stream_rows = place_frames(incoming, arrived, frame_count)
    wide = lax.all_gather(stream_rows, "head", axis=1, tiled=True)
    token_count = wide.shape[0]
    local_heads = w_dt.shape[1]
    groups = w_b.shape[1] // STATE
    per_group = local_heads // groups
    projected_rows = project(wide, norm_gain, w_x, w_b, w_c, w_dt, dt_bias, a_log)
    stretch_count = token_count // STRETCH
    sliced = tuple(
        (member.reshape(stretch_count, STRETCH, member.shape[1]) for member in projected_rows)
    )

    def stretch_step(state, pieces):
        outputs, new_state, cumul = ssd_stretch(
            pieces[0], pieces[1], pieces[2], pieces[3], pieces[4], d_skip, state
        )
        return (new_state, (outputs, cumul))

    zero_state = jnp.zeros((local_heads, HDIM, STATE), jnp.float32)
    device_state, (outputs, cumul) = lax.scan(stretch_step, zero_state, sliced)
    totals = cumul[:, -1, :]
    total_log = jnp.sum(totals, axis=0)
    identity = (jnp.zeros_like(total_log), jnp.zeros_like(device_state))
    incoming_state = carried_in((total_log, device_state), "tm", combine_states, identity)[1]
    offsets = jnp.cumsum(totals, axis=0) - totals
    from_start = (cumul + offsets[:, None, :]).reshape(token_count, local_heads)
    readers = projected_rows[2].astype(jnp.float32).reshape(token_count, groups, STATE)
    correction = (
        jnp.einsum(
            "tgn,gkpn->tgkp",
            readers,
            incoming_state.reshape(groups, per_group, HDIM, STATE),
            precision=highest,
        ).reshape(token_count, local_heads, HDIM)
        * jnp.exp(from_start)[:, :, None]
    )
    combined = outputs.reshape(token_count, local_heads, HDIM) + correction
    return (stream_rows, group_norm(combined, out_gain, groups))


def solution(mesh):
    in_specs = (
        P("tm", None, "head"),
        P("tm"),
        P("tm"),
        P(),
        P(None, None, "head"),
        P("head", None),
        P(None, "head"),
        P(),
        P(None, "head"),
        P(None, "head"),
        P(None, "head"),
        P(None, "head"),
        P("head"),
        P("head"),
        P("head"),
        P("head"),
    )
    out_specs = (P("tm", "head"), P("tm", "head"))
    return jax.shard_map(
        on_device, mesh=mesh, in_specs=in_specs, out_specs=out_specs, check_vma=False
    )
```

profile of v0, /device:TPU:0, one launch (start us, length us, event | category | flops | bytes accessed | tf_op | source)
XLA Modules:
  0.0 784.5 jit_solution(12642048657780200994)
XLA Ops:
  8.7 21.5 %all-gather.6.cloned.1.call-done = bf16[12,256,1152]{1,2,0:T(8,128)(2,1)} async-done(((bf16[12,256,576]{1,2,0:T(8,128)(2,1)}), bf16[12,256,1152]{1,2,0:T(8,128)(2,1)}) %all-gather.6.cloned.1.call-update) | async-done | bytes 7077904 | tf_op jit(solution)/shard_map/all_gather | solution.py:181
  30.2 10.3 %copy.121 = bf16[12,256,1152]{2,1,0:T(8,128)(2,1)} copy(bf16[12,256,1152]{1,2,0:T(8,128)(2,1)} %all-gather.6.cloned.1.call-done) | data formatting | bytes 14155776 | tf_op jit(solution)/shard_map/all_gather | solution.py:181
  40.5 4.2 convert_reduce_fusion
  50.0 15.7 %convert_bitcast_fusion = bf16[3,3072,576]{1,2,0:T(8,128)(2,1)S(1)} fusion(bf16[3072,1152,1]{1,0,2:T(8,128)(2,1)S(1)} %bitcast.239, bf16[3,1152,576]{1,2,0:T(8,128)(2,1)} %param.24), kind=kOutput, calls=%fused_computation.52 | convolution fusion | flops 12235898880 | bytes 21676032 | tf_op jit(solution)/shard_map/rc,mcd->mrd/dot_general | solution.py:50
  65.7 4.1 fusion.96
  69.9 7.2 squeeze.32
  77.1 7.3 squeeze.33
  84.5 7.2 squeeze.31
  91.7 15.7 %fusion.97 = f32[12,8,256]{2,1,0:T(8,128)S(1)} fusion(pred[12,256]{1,0:T(8,128)(4,1)S(1)} %iota_compare_fusion.1, bf16[12,256,8,72]{1,0,3,2:T(8,128)(2,1)} %squeeze.33, bf16[12,256,8,72]{1,0,3,2:T(8,128)(2,1)} %squeeze.32), kind=kOutput, calls=%fused_computation.120 | convolution fusion | flops 931135744 | bytes 7179264 | tf_op jit(solution)/shard_map/sub | solution.py:60
  107.4 21.9 %convert_bitcast_fusion.1 = bf16[12,256,8,72]{1,3,2,0:T(8,128)(2,1)} fusion(f32[12,8,256]{2,1,0:T(8,128)S(1)} %fusion.97, pred[12,256]{1,0:T(8,128)(4,1)S(1)} %iota_compare_fusion.1, bf16[12,256,8,72]{1,0,3,2:T(8,128)(2,1)} %squeeze.31, bf16[12,256,8,72]{1,0,3,2:T(8,128)(2,1)} %squeeze.33, bf16[12,256,8,72]{1,0,3,2:T(8,128)(2,1)} %squeeze.32), kind=kOutput, calls=%fused_computation.71 | convolution fusion | flops 1845190912 | bytes 14257152 | tf_op jit(solution)/shard_map/fhqk,fkhd->fqhd/dot_general | solution.py:62
  129.3 8.0 %copy.126 = bf16[12,256,8,72]{3,2,1,0:T(8,128)(2,1)} copy(bf16[12,256,8,72]{1,3,2,0:T(8,128)(2,1)} %convert_bitcast_fusion.1) | data formatting | bytes 7077888 | tf_op jit(solution)/shard_map/convert_element_type | solution.py:64
  137.3 11.6 %dot_general.53 = bf16[12,64,4,576]{3,2,1,0:T(4,128)(2,1)} reshape(bf16[12,256,8,72]{3,2,1,0:T(8,128)(2,1)} %copy.126) | data formatting | bytes 7077888 | tf_op jit(solution)/shard_map/dot_general | solution.py:65
  148.9 8.6 %fusion.49 = f32[12,64,1152]{2,1,0:T(8,128)S(1)} fusion(bf16[12,64,4,576]{3,2,1,0:T(4,128)(2,1)} %dot_general.53, bf16[576,1152]{1,0:T(8,128)(2,1)S(1)} %copy-done), kind=kOutput, calls=%fused_computation.74 | convolution fusion | flops 4079517696 | bytes 8404992 | tf_op jit(solution)/shard_map/dot_general | solution.py:65
  160.7 6.8 all-to-all-start
  167.5 14.0 %reshape.268 = f32[12,64,4,1152]{3,2,1,0:T(4,128)} reshape(bf16[12,256,1152]{2,1,0:T(8,128)(2,1)} %copy.121) | data formatting | bytes 21233664 | tf_op jit(solution)/shard_map/reshape | solution.py:188
  181.5 13.0 %reduce_sum.89 = f32[12,64,1152]{2,1,0:T(8,128)} reduce(f32[12,64,4,1152]{3,2,1,0:T(4,128)} %reshape.268, f32[]{:T(128)} %constant.94.clone.1), dimensions={2}, to_apply=%region_1.0 | reduce | flops 2654208 | bytes 17694724 | tf_op jit(solution)/shard_map/reduce_sum | solution.py:187
  194.5 3.5 select_convert_fusion
  198.0 6.9 convolution_convert_fusion.1
  207.2 4.3 copy.129
  211.5 7.0 all-to-all-start.1
  218.9 79.3 %all-to-all-done.1 = bf16[16,64,2048]{2,1,0:T(8,128)(2,1)} async-done(((bf16[16,64,2048]{2,1,0:T(8,128)(2,1)}), bf16[16,64,2048]{2,1,0:T(8,128)(2,1)}, u32[]{:S(2)}, u32[]{:S(2)}) %all-to-all-start.1) | async-done | bytes 4194336 | tf_op jit(solution)/shard_map/all_to_all | solution.py:201
  298.2 7.0 fusion.41
  305.2 3.4 copy.131
  308.9 31.1 %all-gather.8.cloned.1.call-done = bf16[768,4096]{1,0:T(8,128)(2,1)} async-done(((bf16[768,2048]{1,0:T(8,128)(2,1)}), bf16[768,4096]{1,0:T(8,128)(2,1)}) %all-gather.8.cloned.1.call-update) | async-done | bytes 6291472 | tf_op jit(solution)/shard_map/all_gather | solution.py:205
  340.0 4.2 fusion.19
  346.9 8.5 %convolution_convert_fusion.2 = bf16[768,512]{1,0:T(8,128)(2,1)} fusion(bf16[4096,512]{1,0:T(8,128)(2,1)} %param.30, bf16[768,4096]{1,0:T(8,128)(2,1)} %all-gather.8.cloned.1.call-done, f32[4096]{0:T(1024)S(1)} %copy-done.13, f32[768]{0:T(1024)S(1)} %add_rsqrt_fusion.2), kind=kOutput, calls=%fused_computation.83 | convolution fusion | flops 3234201600 | bytes 11291648 | tf_op jit(solution)/shard_map/dot_general | solution.py:101
  355.4 4.4 convolution_convert_fusion.3
  359.8 17.9 %convolution_convert_fusion = bf16[768,2048]{1,0:T(8,128)(2,1)} fusion(bf16[4096,2048]{1,0:T(8,128)(2,1)} %param.28, bf16[768,4096]{1,0:T(8,128)(2,1)S(1)} %bitcast.241, f32[4096]{0:T(1024)S(1)} %copy-done.13, f32[768]{0:T(1024)S(1)} %add_rsqrt_fusion.2), kind=kOutput, calls=%fused_computation.72 | convolution fusion | flops 12899057664 | bytes 26233856 | tf_op jit(solution)/shard_map/dot_general | solution.py:99
  377.8 225.2 %while.29 = (s32[]{:T(128)}, f32[32,64,128]{2,1,0:T(8,128)}, f32[3,256,32,64]{1,0,3,2:T(4,128)}, f32[3,256,32]{1,2,0:T(8,128)}, f32[3,256,32]{1,0,2:T(4,128)S(1)...) while((s32[]{:T(128)}, f32[32,64,128]{2,1,0:T(8,128)}, ...), condition=%wide.region_12.13_spmd.clone, body=%wide.region_9.12_spmd.clone.sunk | while | flops 3302842368 | bytes 56987660 | solution.py:223
  384.0 2.9 fusion.146
  396.3 8.0 %fusion.149 = f32[1,256,32,64]{1,3,2,0:T(8,128)S(1)} fusion(f32[256,32,64]{0,2,1:T(8,128)S(1)} %bitcast.224, f32[4,256,8,64]{1,3,2,0:T(8,128)S(1)} %fusion.147, f32[32,256,256]{2,1,0:T(8,128)S(1)} %bitcast_multiply_fusion.4, f32[32]{0:T(128)S(1)} %get-tuple-element.461, f32[256,32]{0,1:T(8,128)S(1)} %get-tuple-element.420, f32[256,32]{0,1:T(8,128)S(1)} %bitcast.238), kind=kOutput, calls=%fused_computation.12.clone.1 | convolution fusion | flops 1613234176 | bytes 14745728 | tf_op jit(solution)/shard_map/while/body/eval_jaxpr/hts,shp->thp/dot_general | solution.py:123
  406.5 45.6 %dynamic_update_slice.14 = f32[3,256,32,64]{1,0,3,2:T(4,128)} dynamic-update-slice(f32[3,256,32,64]{1,0,3,2:T(4,128)} %get-tuple-element.441, f32[1,256,32,64]{1,0,3,2:T(1,128)S(1)} %copy.261, s32[]{:T(128)} %get-tuple-element.439, s32[]{:T(128)} %constant.88.clone.1..sunk, s32[]{:T(128)} %constant.88.clone.1..sunk, s32[]{:T(128)} %constant.88.clone.1..sunk) | dynamic-update-slice | bytes 4194308 | tf_op jit(solution)/shard_map/while/body/jit(dynamic_update_index_in_dim)/dynamic_update_slice | solution.py:223
  458.7 2.9 fusion.146
  461.6 2.7 bitcast_add_fusion.2
  471.3 8.0 %fusion.149 = f32[1,256,32,64]{1,3,2,0:T(8,128)S(1)} fusion(f32[256,32,64]{0,2,1:T(8,128)S(1)} %bitcast.224, f32[4,256,8,64]{1,3,2,0:T(8,128)S(1)} %fusion.147, f32[32,256,256]{2,1,0:T(8,128)S(1)} %bitcast_multiply_fusion.4, f32[32]{0:T(128)S(1)} %get-tuple-element.461, f32[256,32]{0,1:T(8,128)S(1)} %get-tuple-element.420, f32[256,32]{0,1:T(8,128)S(1)} %bitcast.238), kind=kOutput, calls=%fused_computation.12.clone.1 | convolution fusion | flops 1613234176 | bytes 14745728 | tf_op jit(solution)/shard_map/while/body/eval_jaxpr/hts,shp->thp/dot_general | solution.py:123
  481.5 45.6 %dynamic_update_slice.14 = f32[3,256,32,64]{1,0,3,2:T(4,128)} dynamic-update-slice(f32[3,256,32,64]{1,0,3,2:T(4,128)} %get-tuple-element.441, f32[1,256,32,64]{1,0,3,2:T(1,128)S(1)} %copy.261, s32[]{:T(128)} %get-tuple-element.439, s32[]{:T(128)} %constant.88.clone.1..sunk, s32[]{:T(128)} %constant.88.clone.1..sunk, s32[]{:T(128)} %constant.88.clone.1..sunk) | dynamic-update-slice | bytes 4194308 | tf_op jit(solution)/shard_map/while/body/jit(dynamic_update_index_in_dim)/dynamic_update_slice | solution.py:223
  533.6 2.9 fusion.146
  546.3 8.0 %fusion.149 = f32[1,256,32,64]{1,3,2,0:T(8,128)S(1)} fusion(f32[256,32,64]{0,2,1:T(8,128)S(1)} %bitcast.224, f32[4,256,8,64]{1,3,2,0:T(8,128)S(1)} %fusion.147, f32[32,256,256]{2,1,0:T(8,128)S(1)} %bitcast_multiply_fusion.4, f32[32]{0:T(128)S(1)} %get-tuple-element.461, f32[256,32]{0,1:T(8,128)S(1)} %get-tuple-element.420, f32[256,32]{0,1:T(8,128)S(1)} %bitcast.238), kind=kOutput, calls=%fused_computation.12.clone.1 | convolution fusion | flops 1613234176 | bytes 14745728 | tf_op jit(solution)/shard_map/while/body/eval_jaxpr/hts,shp->thp/dot_general | solution.py:123
  556.5 45.6 %dynamic_update_slice.14 = f32[3,256,32,64]{1,0,3,2:T(4,128)} dynamic-update-slice(f32[3,256,32,64]{1,0,3,2:T(4,128)} %get-tuple-element.441, f32[1,256,32,64]{1,0,3,2:T(1,128)S(1)} %copy.261, s32[]{:T(128)} %get-tuple-element.439, s32[]{:T(128)} %constant.88.clone.1..sunk, s32[]{:T(128)} %constant.88.clone.1..sunk, s32[]{:T(128)} %constant.88.clone.1..sunk) | dynamic-update-slice | bytes 4194308 | tf_op jit(solution)/shard_map/while/body/jit(dynamic_update_index_in_dim)/dynamic_update_slice | solution.py:223
  613.2 43.0 %all-reduce = bf16[512]{0:T(512)(128)(2,1)S(1)} all-reduce(bf16[512]{0:T(512)(128)(2,1)S(1)} %dynamic-update-slice), channel_id=2, replica_groups=mesh['tm'=16,'head'=2] {'tm'}, use_global_device_ids=true, to_apply=%add | all-reduce | flops 512 | bytes 2048
  656.3 7.6 copy.176
  663.9 55.5 %all-gather.10.cloned.1.call-done = bf16[512,64,128]{2,1,0:T(8,128)(2,1)} async-done(((bf16[32,64,128]{2,1,0:T(8,128)(2,1)}), bf16[512,64,128]{2,1,0:T(8,128)(2,1)}) %all-gather.10.cloned.1.call-update) | async-done | bytes 8388624 | tf_op jit(solution)/shard_map/all_gather | solution.py:18
  719.4 21.4 %while.30 = (s32[]{:T(128)}, f32[32,64,128]{2,1,0:T(8,128)S(1)}, s32[]{:T(128)}, bf16[16,32]{1,0:T(8,128)(2,1)S(1)}, bf16[16,32,64,128]{3,2,1,0:T(8,128)(2,1)}, /*index=5*/s32[]{:T(128)}, s32[]{:T(128)}) while((s32[]{:T(128)}, f32[32,64,128]{2,1,0:T(8,128)S(1)}, s32[]{:T(128)}, bf16[16,32]{1,0:T(8,128)(2,1)S(1)}, ...), condition=%wide.region_15.16_spmd.clone, body=%wide.region_14.15_spmd.clone.sunk | while | flops 1310756 | bytes 2621865 | solution.py:35
  740.8 4.4 fusion.76
  745.3 10.7 %reshape.282 = f32[3,256,32,64]{1,0,3,2:T(4,128)} reshape(f32[768,4,8,64]{0,3,2,1:T(8,128)} %bitcast.226) | data formatting | bytes 12582912 | tf_op jit(solution)/shard_map/reshape | solution.py:237
  756.0 10.0 %multiply_reduce_fusion.1 = f32[3,256,32]{1,0,2:T(4,128)S(1)} fusion(f32[3,256,32,64]{1,0,3,2:T(4,128)} %get-tuple-element.150, f32[3,256,32,64]{1,0,3,2:T(4,128)} %reshape.282, f32[3,256,32]{1,0,2:T(4,128)S(1)} %copy.139), kind=kLoop, calls=%fused_computation.54 | loop fusion | flops 6266880 | bytes 12779520 | tf_op jit(solution)/shard_map/reduce_sum | solution.py:152
  766.2 7.0 fusion.29
  773.1 4.6 copy.142
  (206 shorter events, 98.1 us)
Async XLA Ops:
  7.2 141.8 %copy-start = (bf16[576,1152]{1,0:T(8,128)(2,1)S(1)}, bf16[576,1152]{1,0:T(8,128)(2,1)}, u32[]{:S(2)}) copy-start(bf16[576,1152]{1,0:T(8,128)(2,1)} %param.25) | copy-start | bytes 3981316
  7.2 23.0 %all-gather.6.cloned.1.call-start = ((), (), s32[]{:S(2)}) async-start(), calls=%async_computation.2 | async-start | bytes 10616832 | tf_op jit(solution)/shard_map/all_gather | solution.py:181
  7.9 186.6 %all-reduce.3.cloned.1.call-start = ((), (), s32[]{:S(2)}) async-start(), calls=%async_computation.3 | async-start | bytes 7077888 | tf_op jit(solution)/shard_map/psum | solution.py:186
  40.5 5.0 copy-start.2
  40.5 7.1 copy-start.10
  157.6 2.3 copy-start.14
  160.7 50.9 %all-to-all-start = ((s32[16,1,1]{2,1,0:T(1,128)}), s32[16,1,1]{2,1,0:T(1,128)S(1)}, u32[]{:S(2)}, u32[]{:S(2)}) async-start(s32[16,1,1]{2,1,0:T(1,128)} %copy.120), calls=%async_computation | async-start | bytes 16384 | tf_op jit(solution)/shard_map/all_to_all | solution.py:202
  211.5 86.7 %all-to-all-start.1 = ((bf16[16,64,2048]{2,1,0:T(8,128)(2,1)}), bf16[16,64,2048]{2,1,0:T(8,128)(2,1)}, u32[]{:S(2)}, u32[]{:S(2)}) async-start(bf16[16,64,2048]{2,1,0:T(8,128)(2,1)} %copy.129), calls=%async_computation.1 | async-start | bytes 8388608 | tf_op jit(solution)/shard_map/all_to_all | solution.py:201
  218.5 121.5 %all-gather.8.cloned.1.call-start = ((), (), s32[]{:S(2)}) async-start(), calls=%async_computation.4 | async-start | bytes 9437184 | tf_op jit(solution)/shard_map/all_gather | solution.py:205
  305.2 3.7 copy-start.15
  308.6 35.7 %copy-start.12 = (bf16[4096,32]{0,1:T(8,128)(2,1)S(1)}, bf16[4096,32]{0,1:T(8,128)(2,1)}, u32[]{:S(2)}) copy-start(bf16[4096,32]{0,1:T(8,128)(2,1)} %param.31) | copy-start | bytes 786436
  308.6 35.7 %copy-start.13 = (f32[4096]{0:T(1024)S(1)}, f32[4096]{0:T(1024)}, u32[]{:S(2)}) copy-start(f32[4096]{0:T(1024)} %param.27) | copy-start | bytes 49156
  308.6 35.7 %copy-start.16 = (f32[32]{0:T(128)S(1)}, f32[32]{0:T(128)}, u32[]{:S(2)}) copy-start(f32[32]{0:T(128)} %param.32) | copy-start | bytes 388
  308.6 410.8 %all-gather.10.cloned.1.call-start = ((), (), s32[]{:S(2)}) async-start(), calls=%async_computation.5 | async-start | bytes 8912896 | tf_op jit(solution)/shard_map/all_gather | solution.py:18
  340.0 4.6 copy-start.3
  344.6 10.8 %slice-start = ((s8[6291456]{0:T(1024)(128)(4,1)}), s8[2097152]{0:T(1024)(128)(4,1)S(1)}, s32[]{:S(2)}) async-start(s8[6291456]{0:T(1024)(128)(4,1)} %bitcast.240), calls=%async_computation.6 | async-start | bytes 4194304
  346.9 8.5 %slice-start.1 = ((s8[6291456]{0:T(1024)(128)(4,1)}), s8[4194304]{0:T(1024)(128)(4,1)S(1)}, s32[]{:S(2)}) async-start(s8[6291456]{0:T(1024)(128)(4,1)} %bitcast.240), calls=%async_computation.7 | async-start | bytes 8388608
  346.9 8.5 %copy-start.11 = (bf16[4096,512]{1,0:T(8,128)(2,1)S(1)}, bf16[4096,512]{1,0:T(8,128)(2,1)}, u32[]{:S(2)}) copy-start(bf16[4096,512]{1,0:T(8,128)(2,1)} %param.29) | copy-start | bytes 12582916
  359.8 17.9 %copy-start.8 = (f32[32]{0:T(128)S(1)}, f32[32]{0:T(128)}, u32[]{:S(2)}) copy-start(f32[32]{0:T(128)} %param.34) | copy-start | bytes 388
  378.2 1.9 copy-start.6
  378.2 3.6 copy-start.4
  404.4 48.5 %copy-start.5 = (f32[3,256,32]{1,0,2:T(4,128)S(1)}, f32[3,256,32]{1,0,2:T(4,128)}, u32[]{:S(2)}) copy-start(f32[3,256,32]{1,0,2:T(4,128)} %copy-done.4) | copy-start | bytes 294916 | tf_op jit(solution)/shard_map/while
  404.4 48.5 %copy-start.7 = (f32[3,256,32]{1,0,2:T(4,128)S(1)}, f32[3,256,32]{1,0,2:T(4,128)}, u32[]{:S(2)}) copy-start(f32[3,256,32]{1,0,2:T(4,128)} %copy-done.6) | copy-start | bytes 294916 | tf_op jit(solution)/shard_map/while
  452.9 1.9 copy-start.6
  452.9 3.6 copy-start.4
  479.3 48.5 %copy-start.5 = (f32[3,256,32]{1,0,2:T(4,128)S(1)}, f32[3,256,32]{1,0,2:T(4,128)}, u32[]{:S(2)}) copy-start(f32[3,256,32]{1,0,2:T(4,128)} %copy-done.4) | copy-start | bytes 294916 | tf_op jit(solution)/shard_map/while
  479.3 48.5 %copy-start.7 = (f32[3,256,32]{1,0,2:T(4,128)S(1)}, f32[3,256,32]{1,0,2:T(4,128)}, u32[]{:S(2)}) copy-start(f32[3,256,32]{1,0,2:T(4,128)} %copy-done.6) | copy-start | bytes 294916 | tf_op jit(solution)/shard_map/while
  527.8 1.9 copy-start.6
  527.8 3.6 copy-start.4
  554.3 48.5 %copy-start.5 = (f32[3,256,32]{1,0,2:T(4,128)S(1)}, f32[3,256,32]{1,0,2:T(4,128)}, u32[]{:S(2)}) copy-start(f32[3,256,32]{1,0,2:T(4,128)} %copy-done.4) | copy-start | bytes 294916 | tf_op jit(solution)/shard_map/while
  554.3 48.5 %copy-start.7 = (f32[3,256,32]{1,0,2:T(4,128)S(1)}, f32[3,256,32]{1,0,2:T(4,128)}, u32[]{:S(2)}) copy-start(f32[3,256,32]{1,0,2:T(4,128)} %copy-done.6) | copy-start | bytes 294916 | tf_op jit(solution)/shard_map/while
  756.0 10.1 %copy-start.9 = (f32[2048]{0:T(1024)S(1)}, f32[2048]{0:T(1024)}, u32[]{:S(2)}) copy-start(f32[2048]{0:T(1024)} %param.35) | copy-start | bytes 24580
  766.2 11.6 %copy-start.1 = (bf16[576,1152]{1,0:T(8,128)(2,1)S(1)}, bf16[576,1152]{1,0:T(8,128)(2,1)}, u32[]{:S(2)}) copy-start(bf16[576,1152]{1,0:T(8,128)(2,1)} %param.25) | copy-start | bytes 3981316
Sparse Core Ops, SparseCore 0:
  9.5 20.6 all-gather.5
  159.9 25.2 all-reduce.2
  308.7 31.2 all-gather.7
  605.2 114.1 all-gather.9
where the time goes:
time: 799 us; the launch traced here: 784 us
  local copies, waits for them, and re-layouts  267 us (33%)
  waiting for transfers between devices  188 us (24%)
  matrix products  158 us (20%)
  other arithmetic  97.5 us (12%)
  blocking collectives  43 us (5%)
  between operations  15 us (2%)
  starting transfers between devices  14.1 us (2%)
    dynamic_update_slice x6, local copies, waits for them, and re-layouts, on_device(): device_state, (outputs, cumul) = lax.scan(stretch_step, zero_state, sliced)  143 us
    all_to_all x1, waiting for transfers between devices, on_device(): lax.all_to_all(outgoing, 'tm', split_axis=0, concat_axis=0, tiled=True)  79.3 us
    all_gather x1, waiting for transfers between devices, carried_in(): lax.all_gather(part.astype(kind), axis)  55.5 us
    unnamed x1, blocking collectives  43 us
    all_gather x1, waiting for transfers between devices, on_device(): wide = lax.all_gather(stream_rows, 'head', axis=1, tiled=True)  31.1 us
    dot_general x3, matrix products, ssd_stretch(): within = jnp.einsum('hts,shp->thp', mixing, scaled, precision=highest)  24 us
    dot_general x1, matrix products, attend(): jnp.einsum('fhqk,fkhd->fqhd', weights_soft, triple[2], preferred_element_...  21.9 us
    all_gather x1, waiting for transfers between devices, on_device(): full_patches = lax.all_gather(patches, 'head', axis=2, tiled=True)  21.5 us
  transfers between devices with their start and end apart: 6, of which 4 were waited for; matrix products, arithmetic and copies ran while one was open for 8% of the time, Pallas kernels for 0%

commit v1 on v0

--- a/solution.py
+++ b/solution.py
@@ -10,6 +10,22 @@
 STATE = 128
 STRETCH = 256
 highest = lax.Precision.HIGHEST
+
+
+def exchange_in_pairs(x, axis, split, join):
+    ways, here = (lax.axis_size(axis), lax.axis_index(axis))
+    width = x.shape[split] // ways
+    shape = list(x.shape)
+    shape[split] = width
+    height = shape[join]
+    shape[join] = height * ways
+    full = jnp.zeros(shape, x.dtype)
+    for mask in range(ways):
+        part = lax.dynamic_slice_in_dim(x, (here ^ mask) * width, width, axis=split)
+        if mask:
+            part = lax.ppermute(part, axis, [(d, d ^ mask) for d in range(ways)])
+        full = lax.dynamic_update_slice_in_dim(full, part, (here ^ mask) * height, axis=join)
+    return full
 
 
 def carried_in(value, axis, combine, identity):
@@ -198,7 +214,7 @@
         projected.reshape(frame_count, tokens_frame, w_conn.shape[1]), frame_ids, shards
     )
     incoming, arrived = (
-        lax.all_to_all(outgoing, "tm", split_axis=0, concat_axis=0, tiled=True),
+        exchange_in_pairs(outgoing, "tm", 0, 0),
         lax.all_to_all(labels, "tm", split_axis=0, concat_axis=0, tiled=True),
     )
     stream_rows = place_frames(incoming, arrived, frame_count)

time: 799 us -> 1100 us (1.38)
  local copies, waits for them, and re-layouts: 267 us -> 442 us
  waiting for transfers between devices: 188 us -> 275 us
  starting transfers between devices: 14.1 us -> 55.3 us
    dynamic_update_slice x0 -> x16, local copies, waits for them, and re-layouts: none -> 163 us  [exchange_in_pairs(): lax.dynamic_update_slice_in_dim(full, part, (here ^ mask) * height, axis=...]
    ppermute x0 -> x15, waiting for transfers between devices: none -> 132 us  [exchange_in_pairs(): part = lax.ppermute(part, axis, [(d, d ^ mask) for d in range(ways)])]
    all_to_all x1 -> x0, waiting for transfers between devices: 79.3 us -> none  [on_device(): lax.all_to_all(outgoing, 'tm', split_axis=0, concat_axis=0, tiled=True)]
    all_to_all x1, waiting for transfers between devices: 0.01 us -> 49.1 us  [on_device(): lax.all_to_all(labels, 'tm', split_axis=0, concat_axis=0, tiled=True)]
    ppermute x0 -> x15, starting transfers between devices: none -> 37.8 us  [exchange_in_pairs(): part = lax.ppermute(part, axis, [(d, d ^ mask) for d in range(ways)])]
    all_gather x1, waiting for transfers between devices: 31.1 us -> 16.3 us  [on_device(): wide = lax.all_gather(stream_rows, 'head', axis=1, tiled=True)]
    dynamic_slice x0 -> x1, local copies, waits for them, and re-layouts: none -> 13.7 us  [exchange_in_pairs(): part = lax.dynamic_slice_in_dim(x, (here ^ mask) * width, width, axis=split)]
  transfers between devices with their start and end apart: 6 -> 20, of which waited for: 4 -> 12; matrix products, arithmetic and copies ran while one was open for 8% -> 18% of each run, Pallas kernels for 0% -> 0%
where the time goes in v1:
time: 1100 us; the launch traced here: 1080 us
  local copies, waits for them, and re-layouts  442 us (40%)
  waiting for transfers between devices  275 us (25%)
  matrix products  154 us (14%)
  other arithmetic  97.7 us (9%)
  starting transfers between devices  55.3 us (5%)
  blocking collectives  42.9 us (4%)
  between operations  15.1 us (1%)
    dynamic_update_slice x16, local copies, waits for them, and re-layouts, exchange_in_pairs(): lax.dynamic_update_slice_in_dim(full, part, (here ^ mask) * height, axis=...  163 us
    dynamic_update_slice x6, local copies, waits for them, and re-layouts, on_device(): device_state, (outputs, cumul) = lax.scan(stretch_step, zero_state, sliced)  143 us
    ppermute x15, waiting for transfers between devices, exchange_in_pairs(): part = lax.ppermute(part, axis, [(d, d ^ mask) for d in range(ways)])  132 us
    all_gather x1, waiting for transfers between devices, carried_in(): lax.all_gather(part.astype(kind), axis)  55.5 us
    all_to_all x1, waiting for transfers between devices, on_device(): lax.all_to_all(labels, 'tm', split_axis=0, concat_axis=0, tiled=True)  49.1 us
    unnamed x1, blocking collectives  42.9 us
    ppermute x15, starting transfers between devices, exchange_in_pairs(): part = lax.ppermute(part, axis, [(d, d ^ mask) for d in range(ways)])  37.8 us
    dot_general x3, matrix products, ssd_stretch(): within = jnp.einsum('hts,shp->thp', mixing, scaled, precision=highest)  24 us
  transfers between devices with their start and end apart: 20, of which 12 were waited for; matrix products, arithmetic and copies ran while one was open for 18% of the time, Pallas kernels for 0%

profile of v1, /device:TPU:0, one launch (start us, length us, event | category | flops | bytes accessed | tf_op | source)
XLA Modules:
  0.0 1083.7 jit_solution(17535358395331710314)
XLA Ops:
  8.7 21.5 %all-gather.6.cloned.1.call-done = bf16[12,256,1152]{1,2,0:T(8,128)(2,1)} async-done(((bf16[12,256,576]{1,2,0:T(8,128)(2,1)}), bf16[12,256,1152]{1,2,0:T(8,128)(2,1)}) %all-gather.6.cloned.1.call-update) | async-done | bytes 7077904 | tf_op jit(solution)/shard_map/all_gather | solution.py:197
  30.2 10.3 copy.121
  50.0 15.7 %convert_bitcast_fusion = bf16[3,3072,576]{1,2,0:T(8,128)(2,1)S(1)} fusion(bf16[3072,1152,1]{1,0,2:T(8,128)(2,1)S(1)} %bitcast.240, bf16[3,1152,576]{1,2,0:T(8,128)(2,1)} %param.24), kind=kOutput, calls=%fused_computation.52 | convolution fusion | flops 12235898880 | bytes 21676032 | tf_op jit(solution)/shard_map/rc,mcd->mrd/dot_general | solution.py:66
  91.7 15.7 %fusion.92 = f32[12,8,256]{2,1,0:T(8,128)S(1)} fusion(pred[12,256]{1,0:T(8,128)(4,1)S(1)} %iota_compare_fusion.1, bf16[12,256,8,72]{1,0,3,2:T(8,128)(2,1)} %squeeze.33, bf16[12,256,8,72]{1,0,3,2:T(8,128)(2,1)} %squeeze.32), kind=kOutput, calls=%fused_computation.134 | convolution fusion | flops 931135744 | bytes 7179264 | tf_op jit(solution)/shard_map/sub | solution.py:76
  107.4 21.9 %convert_bitcast_fusion.1 = bf16[12,256,8,72]{1,3,2,0:T(8,128)(2,1)} fusion(f32[12,8,256]{2,1,0:T(8,128)S(1)} %fusion.92, pred[12,256]{1,0:T(8,128)(4,1)S(1)} %iota_compare_fusion.1, bf16[12,256,8,72]{1,0,3,2:T(8,128)(2,1)} %squeeze.31, bf16[12,256,8,72]{1,0,3,2:T(8,128)(2,1)} %squeeze.33, bf16[12,256,8,72]{1,0,3,2:T(8,128)(2,1)} %squeeze.32), kind=kOutput, calls=%fused_computation.69 | convolution fusion | flops 1845190912 | bytes 14257152 | tf_op jit(solution)/shard_map/fhqk,fkhd->fqhd/dot_general | solution.py:78
  129.3 8.0 copy.126
  137.3 11.6 %dot_general.53 = bf16[12,64,4,576]{3,2,1,0:T(4,128)(2,1)} reshape(bf16[12,256,8,72]{3,2,1,0:T(8,128)(2,1)} %copy.126) | data formatting | bytes 7077888 | tf_op jit(solution)/shard_map/dot_general | solution.py:81
  148.9 8.6 fusion.44
  160.0 13.9 %reshape.268 = f32[12,64,4,1152]{3,2,1,0:T(4,128)} reshape(bf16[12,256,1152]{2,1,0:T(8,128)(2,1)} %copy.121) | data formatting | bytes 21233664 | tf_op jit(solution)/shard_map/reshape | solution.py:204
  174.0 13.2 %reduce_sum.89 = f32[12,64,1152]{2,1,0:T(8,128)} reduce(f32[12,64,4,1152]{3,2,1,0:T(4,128)} %reshape.268, f32[]{:T(128)} %constant.111.clone.1), dimensions={2}, to_apply=%region_1.0 | reduce | flops 2654208 | bytes 17694724 | tf_op jit(solution)/shard_map/reduce_sum | solution.py:203
  200.0 13.7 %constant_dynamic-slice_fusion.5 = (bf16[1,64,2048]{2,0,1:T(2,128)(2,1)}, bf16[1,64,2048]{2,0,1:T(2,128)(2,1)}, bf16[1,64,2048]{2,0,1:T(2,128)(2,1)}, bf16[1,64,...) fusion(bf16[16,64,2048]{2,0,1:T(8,128)(2,1)S(1)} %fusion.36, ...), kind=kLoop, calls=%fused_computation.107 | loop fusion | bytes 8388672 | tf_op jit(solution)/shard_map/dynamic_slice | solution.py:24
  220.3 8.1 collective-permute-done
  233.0 25.0 %collective-permute-done.2 = bf16[1,64,2048]{2,0,1:T(2,128)(2,1)S(1)} collective-permute-done((bf16[1,64,2048]{2,0,1:T(2,128)(2,1)S(1)}, bf16[1,64,2048]{2,0,1:T(2,128)(2,1)S(1)}, u32[]{:S(2)}, u32[]{:S(2)}) %collective-permute-start.2) | collective-permute-done | bytes 262176 | tf_op jit(solution)/shard_map/ppermute | solution.py:26
  264.7 12.2 %collective-permute-done.5 = bf16[1,64,2048]{2,0,1:T(2,128)(2,1)} collective-permute-done((bf16[1,64,2048]{2,0,1:T(2,128)(2,1)S(1)}, bf16[1,64,2048]{2,0,1:T(2,128)(2,1)}, u32[]{:S(2)}, u32[]{:S(2)}) %collective-permute-start.5) | collective-permute-done | bytes 262176 | tf_op jit(solution)/shard_map/ppermute | solution.py:26
  276.9 10.2 collective-permute-done.6
  288.6 47.0 %collective-permute-done.7 = bf16[1,64,2048]{2,0,1:T(2,128)(2,1)} collective-permute-done((bf16[1,64,2048]{2,0,1:T(2,128)(2,1)S(1)}, bf16[1,64,2048]{2,0,1:T(2,128)(2,1)}, u32[]{:S(2)}, u32[]{:S(2)}) %collective-permute-start.7) | collective-permute-done | bytes 262176 | tf_op jit(solution)/shard_map/ppermute | solution.py:26
  340.3 25.2 %collective-permute-done.8 = bf16[1,64,2048]{2,0,1:T(2,128)(2,1)} collective-permute-done((bf16[1,64,2048]{2,0,1:T(2,128)(2,1)S(1)}, bf16[1,64,2048]{2,0,1:T(2,128)(2,1)}, u32[]{:S(2)}, u32[]{:S(2)}) %collective-permute-start.8) | collective-permute-done | bytes 262176 | tf_op jit(solution)/shard_map/ppermute | solution.py:26
  368.9 14.3 %collective-permute-start.14 = (bf16[1,64,2048]{2,0,1:T(2,128)(2,1)}, bf16[1,64,2048]{2,0,1:T(2,128)(2,1)}, u32[]{:S(2)}, u32[]{:S(2)}) collective-permute-start(bf16[1,64,2048]{2,0,1:T(2,128)(2,1)} %get-tuple-element.308), channel_id=1, source_target_pairs={{0,30},{2,28},{4,26},{6,24},{8,22},{10,20},{12,18},{14,16},{16,14}... | collective-permute-start | bytes 786440 | tf_op jit(solution)/shard_map/ppermute | solution.py:26
  384.0 16.9 %all-to-all-start = ((s32[16,1,1]{2,1,0:T(1,128)}), s32[16,1,1]{2,1,0:T(1,128)S(1)}, u32[]{:S(2)}, u32[]{:S(2)}) async-start(s32[16,1,1]{2,1,0:T(1,128)} %copy.120), calls=%async_computation | async-start | bytes 16384 | tf_op jit(solution)/shard_map/all_to_all | solution.py:218
  400.9 49.1 %all-to-all-done = s32[16,1,1]{2,1,0:T(1,128)S(1)} async-done(((s32[16,1,1]{2,1,0:T(1,128)}), s32[16,1,1]{2,1,0:T(1,128)S(1)}, u32[]{:S(2)}, u32[]{:S(2)}) %all-to-all-start) | async-done | bytes 96 | tf_op jit(solution)/shard_map/all_to_all | solution.py:218
  452.9 10.2 dynamic_update_slice.56
  463.1 10.2 dynamic_update_slice.57
  473.3 10.2 dynamic_update_slice.58
  483.4 10.2 dynamic_update_slice.59
  493.6 10.2 dynamic_update_slice.60
  503.8 10.2 dynamic_update_slice.61
  513.9 10.2 dynamic_update_slice.62
  524.1 10.2 dynamic_update_slice.63
  534.3 10.2 dynamic_update_slice.64
  544.5 10.2 dynamic_update_slice.65
  554.7 10.2 dynamic_update_slice.66
  564.9 10.2 dynamic_update_slice.67
  575.1 10.2 dynamic_update_slice.68
  585.3 10.2 dynamic_update_slice.69
  595.6 10.2 dynamic_update_slice.70
  605.8 10.2 dynamic_update_slice.71
  623.3 16.3 %all-gather.8.cloned.1.call-done = bf16[768,4096]{1,0:T(8,128)(2,1)} async-done(((bf16[768,2048]{1,0:T(8,128)(2,1)}), bf16[768,4096]{1,0:T(8,128)(2,1)}) %all-gather.8.cloned.1.call-update) | async-done | bytes 6291472 | tf_op jit(solution)/shard_map/all_gather | solution.py:221
  646.5 8.5 convolution_convert_fusion.3
  659.4 17.9 %convolution_convert_fusion.1 = bf16[768,2048]{1,0:T(8,128)(2,1)} fusion(bf16[4096,2048]{1,0:T(8,128)(2,1)} %param.28, bf16[768,4096]{1,0:T(8,128)(2,1)S(1)} %bitcast.242, f32[4096]{0:T(1024)S(1)} %copy-done.13, f32[768]{0:T(1024)S(1)} %add_rsqrt_fusion.2), kind=kOutput, calls=%fused_computation.70 | convolution fusion | flops 12899057664 | bytes 26233856 | tf_op jit(solution)/shard_map/dot_general | solution.py:115
  677.3 224.9 %while.29 = (s32[]{:T(128)}, f32[32,64,128]{2,1,0:T(8,128)}, f32[3,256,32,64]{1,0,3,2:T(4,128)}, f32[3,256,32]{1,2,0:T(8,128)}, f32[3,256,32]{1,0,2:T(4,128)S(1)...) while((s32[]{:T(128)}, f32[32,64,128]{2,1,0:T(8,128)}, ...), condition=%wide.region_12.13_spmd.clone, body=%wide.region_9.12_spmd.clone.sunk | while | flops 3302842368 | bytes 56987660 | solution.py:239
  705.8 45.6 %dynamic_update_slice.78 = f32[3,256,32,64]{1,0,3,2:T(4,128)} dynamic-update-slice(f32[3,256,32,64]{1,0,3,2:T(4,128)} %get-tuple-element.457, f32[1,256,32,64]{1,0,3,2:T(1,128)S(1)} %copy.255, s32[]{:T(128)} %get-tuple-element.455, s32[]{:T(128)} %constant.60.clone.1..sunk, s32[]{:T(128)} %constant.60.clone.1..sunk, s32[]{:T(128)} %constant.60.clone.1..sunk) | dynamic-update-slice | bytes 4194308 | tf_op jit(solution)/shard_map/while/body/jit(dynamic_update_index_in_dim)/dynamic_update_slice | solution.py:239
  780.8 45.6 %dynamic_update_slice.78 = f32[3,256,32,64]{1,0,3,2:T(4,128)} dynamic-update-slice(f32[3,256,32,64]{1,0,3,2:T(4,128)} %get-tuple-element.457, f32[1,256,32,64]{1,0,3,2:T(1,128)S(1)} %copy.255, s32[]{:T(128)} %get-tuple-element.455, s32[]{:T(128)} %constant.60.clone.1..sunk, s32[]{:T(128)} %constant.60.clone.1..sunk, s32[]{:T(128)} %constant.60.clone.1..sunk) | dynamic-update-slice | bytes 4194308 | tf_op jit(solution)/shard_map/while/body/jit(dynamic_update_index_in_dim)/dynamic_update_slice | solution.py:239
  855.7 45.6 %dynamic_update_slice.78 = f32[3,256,32,64]{1,0,3,2:T(4,128)} dynamic-update-slice(f32[3,256,32,64]{1,0,3,2:T(4,128)} %get-tuple-element.457, f32[1,256,32,64]{1,0,3,2:T(1,128)S(1)} %copy.255, s32[]{:T(128)} %get-tuple-element.455, s32[]{:T(128)} %constant.60.clone.1..sunk, s32[]{:T(128)} %constant.60.clone.1..sunk, s32[]{:T(128)} %constant.60.clone.1..sunk) | dynamic-update-slice | bytes 4194308 | tf_op jit(solution)/shard_map/while/body/jit(dynamic_update_index_in_dim)/dynamic_update_slice | solution.py:239
  912.4 42.9 %all-reduce = bf16[512]{0:T(512)(128)(2,1)S(1)} all-reduce(bf16[512]{0:T(512)(128)(2,1)S(1)} %dynamic-update-slice), channel_id=2, replica_groups=mesh['tm'=16,'head'=2] {'tm'}, use_global_device_ids=true, to_apply=%add | all-reduce | flops 512 | bytes 2048
  963.0 55.5 %all-gather.10.cloned.1.call-done = bf16[512,64,128]{2,1,0:T(8,128)(2,1)} async-done(((bf16[32,64,128]{2,1,0:T(8,128)(2,1)}), bf16[512,64,128]{2,1,0:T(8,128)(2,1)}) %all-gather.10.cloned.1.call-update) | async-done | bytes 8388624 | tf_op jit(solution)/shard_map/all_gather | solution.py:34
  1018.6 21.4 %while.30 = (s32[]{:T(128)}, f32[32,64,128]{2,1,0:T(8,128)S(1)}, s32[]{:T(128)}, bf16[16,32]{1,0:T(8,128)(2,1)S(1)}, bf16[16,32,64,128]{3,2,1,0:T(8,128)(2,1)}, /*index=5*/s32[]{:T(128)}, s32[]{:T(128)}) while((s32[]{:T(128)}, f32[32,64,128]{2,1,0:T(8,128)S(1)}, s32[]{:T(128)}, bf16[16,32]{1,0:T(8,128)(2,1)S(1)}, ...), condition=%wide.region_15.16_spmd.clone, body=%wide.region_14.15_spmd.clone.sunk | while | flops 1310756 | bytes 2621865 | solution.py:51
  1044.4 10.7 reshape.282
  1055.2 10.0 multiply_reduce_fusion.1
  (251 shorter events, 243.4 us)
Async XLA Ops:
  7.2 141.8 %copy-start = (bf16[576,1152]{1,0:T(8,128)(2,1)S(1)}, bf16[576,1152]{1,0:T(8,128)(2,1)}, u32[]{:S(2)}) copy-start(bf16[576,1152]{1,0:T(8,128)(2,1)} %param.25) | copy-start | bytes 3981316
  7.2 23.0 %all-gather.6.cloned.1.call-start = ((), (), s32[]{:S(2)}) async-start(), calls=%async_computation.1 | async-start | bytes 10616832 | tf_op jit(solution)/shard_map/all_gather | solution.py:197
  7.9 179.3 %all-reduce.3.cloned.1.call-start = ((), (), s32[]{:S(2)}) async-start(), calls=%async_computation.2 | async-start | bytes 7077888 | tf_op jit(solution)/shard_map/psum | solution.py:202
  40.5 5.0 copy-start.2
  44.7 2.9 copy-start.10
  157.6 2.4 copy-start.14
  213.7 14.8 %collective-permute-start = (bf16[1,64,2048]{2,0,1:T(2,128)(2,1)S(1)}, bf16[1,64,2048]{2,0,1:T(2,128)(2,1)S(1)}, u32[]{:S(2)}, u32[]{:S(2)}) collective-permute-start(bf16[1,64,2048]{2,0,1:T(2,128)(2,1)S(1)} %get-tuple-element.322), channel_id=1, source_target_pairs={{0,2},{2,0},{4,6},{6,4},{8,10},{10,8},{12,14},{14,12},{16,18},{18,... | collective-permute-start | bytes 786440 | tf_op jit(solution)/shard_map/ppermute | solution.py:26
  215.4 16.4 %collective-permute-start.1 = (bf16[1,64,2048]{2,0,1:T(2,128)(2,1)S(1)}, bf16[1,64,2048]{2,0,1:T(2,128)(2,1)S(1)}, u32[]{:S(2)}, u32[]{:S(2)}) collective-permute-start(bf16[1,64,2048]{2,0,1:T(2,128)(2,1)S(1)} %get-tuple-element.321), channel_id=1, source_target_pairs={{0,4},{2,6},{4,0},{6,2},{8,12},{10,14},{12,8},{14,10},{16,20},{18,... | collective-permute-start | bytes 786440 | tf_op jit(solution)/shard_map/ppermute | solution.py:26
  216.9 41.1 %collective-permute-start.2 = (bf16[1,64,2048]{2,0,1:T(2,128)(2,1)S(1)}, bf16[1,64,2048]{2,0,1:T(2,128)(2,1)S(1)}, u32[]{:S(2)}, u32[]{:S(2)}) collective-permute-start(bf16[1,64,2048]{2,0,1:T(2,128)(2,1)S(1)} %get-tuple-element.320), channel_id=1, source_target_pairs={{0,6},{2,4},{4,2},{6,0},{8,14},{10,12},{12,10},{14,8},{16,22},{18,... | collective-permute-start | bytes 786440 | tf_op jit(solution)/shard_map/ppermute | solution.py:26
  217.1 43.3 %collective-permute-start.3 = (bf16[1,64,2048]{2,0,1:T(2,128)(2,1)S(1)}, bf16[1,64,2048]{2,0,1:T(2,128)(2,1)S(1)}, u32[]{:S(2)}, u32[]{:S(2)}) collective-permute-start(bf16[1,64,2048]{2,0,1:T(2,128)(2,1)S(1)} %get-tuple-element.319), channel_id=1, source_target_pairs={{0,8},{2,10},{4,12},{6,14},{8,0},{10,2},{12,4},{14,6},{16,24},{18,... | collective-permute-start | bytes 786440 | tf_op jit(solution)/shard_map/ppermute | solution.py:26
  218.9 43.4 %collective-permute-start.4 = (bf16[1,64,2048]{2,0,1:T(2,128)(2,1)S(1)}, bf16[1,64,2048]{2,0,1:T(2,128)(2,1)S(1)}, u32[]{:S(2)}, u32[]{:S(2)}) collective-permute-start(bf16[1,64,2048]{2,0,1:T(2,128)(2,1)S(1)} %get-tuple-element.318), channel_id=1, source_target_pairs={{0,10},{2,8},{4,14},{6,12},{8,2},{10,0},{12,6},{14,4},{16,26},{18,... | collective-permute-start | bytes 786440 | tf_op jit(solution)/shard_map/ppermute | solution.py:26
  228.5 48.4 %collective-permute-start.5 = (bf16[1,64,2048]{2,0,1:T(2,128)(2,1)S(1)}, bf16[1,64,2048]{2,0,1:T(2,128)(2,1)}, u32[]{:S(2)}, u32[]{:S(2)}) collective-permute-start(bf16[1,64,2048]{2,0,1:T(2,128)(2,1)S(1)} %get-tuple-element.317), channel_id=1, source_target_pairs={{0,12},{2,14},{4,8},{6,10},{8,4},{10,6},{12,0},{14,2},{16,28},{18,... | collective-permute-start | bytes 786440 | tf_op jit(solution)/shard_map/ppermute | solution.py:26
  231.8 55.3 %collective-permute-start.6 = (bf16[1,64,2048]{2,0,1:T(2,128)(2,1)S(1)}, bf16[1,64,2048]{2,0,1:T(2,128)(2,1)}, u32[]{:S(2)}, u32[]{:S(2)}) collective-permute-start(bf16[1,64,2048]{2,0,1:T(2,128)(2,1)S(1)} %get-tuple-element.316), channel_id=1, source_target_pairs={{0,14},{2,12},{4,10},{6,8},{8,6},{10,4},{12,2},{14,0},{16,30},{18,... | collective-permute-start | bytes 786440 | tf_op jit(solution)/shard_map/ppermute | solution.py:26
  258.0 77.6 %collective-permute-start.7 = (bf16[1,64,2048]{2,0,1:T(2,128)(2,1)S(1)}, bf16[1,64,2048]{2,0,1:T(2,128)(2,1)}, u32[]{:S(2)}, u32[]{:S(2)}) collective-permute-start(bf16[1,64,2048]{2,0,1:T(2,128)(2,1)S(1)} %get-tuple-element.315), channel_id=1, source_target_pairs={{0,16},{2,18},{4,20},{6,22},{8,24},{10,26},{12,28},{14,30},{16,0},... | collective-permute-start | bytes 786440 | tf_op jit(solution)/shard_map/ppermute | solution.py:26
  260.4 105.1 %collective-permute-start.8 = (bf16[1,64,2048]{2,0,1:T(2,128)(2,1)S(1)}, bf16[1,64,2048]{2,0,1:T(2,128)(2,1)}, u32[]{:S(2)}, u32[]{:S(2)}) collective-permute-start(bf16[1,64,2048]{2,0,1:T(2,128)(2,1)S(1)} %get-tuple-element.314), channel_id=1, source_target_pairs={{0,18},{2,16},{4,22},{6,20},{8,26},{10,24},{12,30},{14,28},{16,2},... | collective-permute-start | bytes 786440 | tf_op jit(solution)/shard_map/ppermute | solution.py:26
  262.3 106.6 %collective-permute-start.9 = (bf16[1,64,2048]{2,0,1:T(2,128)(2,1)S(1)}, bf16[1,64,2048]{2,0,1:T(2,128)(2,1)}, u32[]{:S(2)}, u32[]{:S(2)}) collective-permute-start(bf16[1,64,2048]{2,0,1:T(2,128)(2,1)S(1)} %get-tuple-element.313), channel_id=1, source_target_pairs={{0,20},{2,22},{4,16},{6,18},{8,28},{10,30},{12,24},{14,26},{16,4},... | collective-permute-start | bytes 786440 | tf_op jit(solution)/shard_map/ppermute | solution.py:26
  276.9 288.1 %collective-permute-start.10 = (bf16[1,64,2048]{2,0,1:T(2,128)(2,1)}, bf16[1,64,2048]{2,0,1:T(2,128)(2,1)}, u32[]{:S(2)}, u32[]{:S(2)}) collective-permute-start(bf16[1,64,2048]{2,0,1:T(2,128)(2,1)} %get-tuple-element.312), channel_id=1, source_target_pairs={{0,22},{2,20},{4,18},{6,16},{8,30},{10,28},{12,26},{14,24},{16,6},... | collective-permute-start | bytes 786440 | tf_op jit(solution)/shard_map/ppermute | solution.py:26
  287.0 288.1 %collective-permute-start.11 = (bf16[1,64,2048]{2,0,1:T(2,128)(2,1)}, bf16[1,64,2048]{2,0,1:T(2,128)(2,1)}, u32[]{:S(2)}, u32[]{:S(2)}) collective-permute-start(bf16[1,64,2048]{2,0,1:T(2,128)(2,1)} %get-tuple-element.311), channel_id=1, source_target_pairs={{0,24},{2,26},{4,28},{6,30},{8,16},{10,18},{12,20},{14,22},{16,8},... | collective-permute-start | bytes 786440 | tf_op jit(solution)/shard_map/ppermute | solution.py:26
  335.6 249.8 %collective-permute-start.12 = (bf16[1,64,2048]{2,0,1:T(2,128)(2,1)}, bf16[1,64,2048]{2,0,1:T(2,128)(2,1)}, u32[]{:S(2)}, u32[]{:S(2)}) collective-permute-start(bf16[1,64,2048]{2,0,1:T(2,128)(2,1)} %get-tuple-element.310), channel_id=1, source_target_pairs={{0,26},{2,24},{4,30},{6,28},{8,18},{10,16},{12,22},{14,20},{16,10}... | collective-permute-start | bytes 786440 | tf_op jit(solution)/shard_map/ppermute | solution.py:26
  365.5 230.1 %collective-permute-start.13 = (bf16[1,64,2048]{2,0,1:T(2,128)(2,1)}, bf16[1,64,2048]{2,0,1:T(2,128)(2,1)}, u32[]{:S(2)}, u32[]{:S(2)}) collective-permute-start(bf16[1,64,2048]{2,0,1:T(2,128)(2,1)} %get-tuple-element.309), channel_id=1, source_target_pairs={{0,28},{2,30},{4,24},{6,26},{8,20},{10,22},{12,16},{14,18},{16,12}... | collective-permute-start | bytes 786440 | tf_op jit(solution)/shard_map/ppermute | solution.py:26
  368.9 236.9 %collective-permute-start.14 = (bf16[1,64,2048]{2,0,1:T(2,128)(2,1)}, bf16[1,64,2048]{2,0,1:T(2,128)(2,1)}, u32[]{:S(2)}, u32[]{:S(2)}) collective-permute-start(bf16[1,64,2048]{2,0,1:T(2,128)(2,1)} %get-tuple-element.308), channel_id=1, source_target_pairs={{0,30},{2,28},{4,26},{6,24},{8,22},{10,20},{12,18},{14,16},{16,14}... | collective-permute-start | bytes 786440 | tf_op jit(solution)/shard_map/ppermute | solution.py:26
  384.0 66.1 %all-to-all-start = ((s32[16,1,1]{2,1,0:T(1,128)}), s32[16,1,1]{2,1,0:T(1,128)S(1)}, u32[]{:S(2)}, u32[]{:S(2)}) async-start(s32[16,1,1]{2,1,0:T(1,128)} %copy.120), calls=%async_computation | async-start | bytes 16384 | tf_op jit(solution)/shard_map/all_to_all | solution.py:218
  400.9 238.7 %all-gather.8.cloned.1.call-start = ((), (), s32[]{:S(2)}) async-start(), calls=%async_computation.3 | async-start | bytes 9437184 | tf_op jit(solution)/shard_map/all_gather | solution.py:221
  619.4 3.9 copy-start.15
  622.8 21.0 %copy-start.12 = (bf16[4096,32]{0,1:T(8,128)(2,1)S(1)}, bf16[4096,32]{0,1:T(8,128)(2,1)}, u32[]{:S(2)}) copy-start(bf16[4096,32]{0,1:T(8,128)(2,1)} %param.31) | copy-start | bytes 786436
  622.8 21.0 %copy-start.13 = (f32[4096]{0:T(1024)S(1)}, f32[4096]{0:T(1024)}, u32[]{:S(2)}) copy-start(f32[4096]{0:T(1024)} %param.27) | copy-start | bytes 49156
  622.8 21.1 %copy-start.16 = (f32[32]{0:T(128)S(1)}, f32[32]{0:T(128)}, u32[]{:S(2)}) copy-start(f32[32]{0:T(128)} %param.32) | copy-start | bytes 388
  622.8 395.7 %all-gather.10.cloned.1.call-start = ((), (), s32[]{:S(2)}) async-start(), calls=%async_computation.4 | async-start | bytes 8912896 | tf_op jit(solution)/shard_map/all_gather | solution.py:34
  639.6 4.6 copy-start.3
  644.2 10.8 slice-start
  646.5 8.5 slice-start.1
  646.5 8.5 copy-start.11
  659.4 17.9 %copy-start.8 = (f32[32]{0:T(128)S(1)}, f32[32]{0:T(128)}, u32[]{:S(2)}) copy-start(f32[32]{0:T(128)} %param.34) | copy-start | bytes 388
  677.5 1.9 copy-start.6
  677.5 3.6 copy-start.4
  703.6 48.5 %copy-start.5 = (f32[3,256,32]{1,0,2:T(4,128)S(1)}, f32[3,256,32]{1,0,2:T(4,128)}, u32[]{:S(2)}) copy-start(f32[3,256,32]{1,0,2:T(4,128)} %copy-done.4) | copy-start | bytes 294916 | tf_op jit(solution)/shard_map/while
  703.6 48.5 %copy-start.7 = (f32[3,256,32]{1,0,2:T(4,128)S(1)}, f32[3,256,32]{1,0,2:T(4,128)}, u32[]{:S(2)}) copy-start(f32[3,256,32]{1,0,2:T(4,128)} %copy-done.6) | copy-start | bytes 294916 | tf_op jit(solution)/shard_map/while
  752.1 1.9 copy-start.6
  752.2 3.6 copy-start.4
  778.6 48.5 %copy-start.5 = (f32[3,256,32]{1,0,2:T(4,128)S(1)}, f32[3,256,32]{1,0,2:T(4,128)}, u32[]{:S(2)}) copy-start(f32[3,256,32]{1,0,2:T(4,128)} %copy-done.4) | copy-start | bytes 294916 | tf_op jit(solution)/shard_map/while
  778.6 48.5 %copy-start.7 = (f32[3,256,32]{1,0,2:T(4,128)S(1)}, f32[3,256,32]{1,0,2:T(4,128)}, u32[]{:S(2)}) copy-start(f32[3,256,32]{1,0,2:T(4,128)} %copy-done.6) | copy-start | bytes 294916 | tf_op jit(solution)/shard_map/while
  827.1 1.9 copy-start.6
  827.1 3.6 copy-start.4
  853.6 48.5 %copy-start.5 = (f32[3,256,32]{1,0,2:T(4,128)S(1)}, f32[3,256,32]{1,0,2:T(4,128)}, u32[]{:S(2)}) copy-start(f32[3,256,32]{1,0,2:T(4,128)} %copy-done.4) | copy-start | bytes 294916 | tf_op jit(solution)/shard_map/while
  853.6 48.5 %copy-start.7 = (f32[3,256,32]{1,0,2:T(4,128)S(1)}, f32[3,256,32]{1,0,2:T(4,128)}, u32[]{:S(2)}) copy-start(f32[3,256,32]{1,0,2:T(4,128)} %copy-done.6) | copy-start | bytes 294916 | tf_op jit(solution)/shard_map/while
  1055.2 10.1 copy-start.9
  1065.3 11.6 %copy-start.1 = (bf16[576,1152]{1,0:T(8,128)(2,1)S(1)}, bf16[576,1152]{1,0:T(8,128)(2,1)}, u32[]{:S(2)}) copy-start(bf16[576,1152]{1,0:T(8,128)(2,1)} %param.25) | copy-start | bytes 3981316
Sparse Core Ops, SparseCore 0:
  9.5 20.6 all-gather.5
  159.9 25.2 all-reduce.2
  622.9 16.6 all-gather.7
  904.5 113.9 all-gather.9
